TPU v7x, 32 devices: a whole 2x2x4 slice. The times are simulated.
32 devices in a mesh: groups: 1, seq: 32 (over z, y, x, core).
Axes of the slice: x: 2, y: 2, z: 4, core: 2. Of those that a mesh axis runs over, the one named last changes fastest.
Arguments:
- q_gate: bfloat16 [4096, 4096], P(('groups', 'seq')), may hold values from -6 to 6
- values_in: bfloat16 [4096, 4096], P(('groups', 'seq')), may hold values from -6 to 6
- decay_rate: float32 [4096, 16], replicated, as said below
- residue: float32 [4096, 16], replicated, may hold values from -3 to 3
- skip_gain: float32 [4096], replicated, may hold values from 0.5 to 1.5
- out_weight: bfloat16 [4096, 2048], P('seq'), may hold values from -0.09375 to 0.09375
Outputs:
- mixed: bfloat16 [4096, 2048], P(('groups', 'seq'))
Inputs may be any that keep to these rules, and one draw needn't show every extreme that they name: `decay_rate`: every rate is positive and at most about 1/30.
All inputs are finite; a program needn't handle non-finite values.
Results may differ from a plain program's by a relative error of at most 0.0052.
Values may be sent and summed in bfloat16 or wider, within the bound.
A program may use at most 256 MiB of HBM per device.

v0:
```python
import jax
import jax.numpy as jnp
from jax import lax
from jax.sharding import PartitionSpec as P

ORDER = 16
BLOCK = 32


def entering(value, axis, join, neutral):
    count, mine = (lax.axis_size(axis), lax.axis_index(axis))
    pieces = jax.tree.map(lambda part: lax.all_gather(part, axis), value)
    running = jax.tree.map(
        lambda part, zero: jnp.full_like(part, 0) + jnp.asarray(zero, part.dtype), value, neutral
    )

    def hop(position, running):
        longer = join(running, jax.tree.map(lambda part: part[position], pieces))
        return jax.tree.map(lambda new, old: jnp.where(position < mine, new, old), longer, running)

    return lax.fori_loop(0, count - 1, hop, running)


def on_device(q_gate, values_in, decay_rate, residue, skip_gain, out_weight):
    tok_rows = q_gate.shape[0]
    width = q_gate.shape[1]
    block_count = tok_rows // BLOCK
    rate_modes = decay_rate.T
    mode_scale = jnp.sqrt(-jnp.expm1(-2.0 * rate_modes))
    mode_coef = residue.T * mode_scale
    position = jnp.arange(BLOCK, dtype=jnp.float32)
    tap_values = jnp.sum(
        mode_coef[None] * jnp.exp(-position[:, None, None] * rate_modes[None]), axis=1
    )
    tap_round = tap_values.astype(jnp.bfloat16)
    offsets = jnp.arange(BLOCK)[:, None] - jnp.arange(BLOCK)[None, :]
    selector = (
        (jnp.arange(BLOCK)[:, None, None] == offsets[None])
        .astype(jnp.bfloat16)
        .reshape(BLOCK, BLOCK * BLOCK)
    )
    toeplitz = jnp.dot(tap_round.T, selector, preferred_element_type=jnp.bfloat16).reshape(
        width, BLOCK, BLOCK
    )
    blocked = values_in.reshape(block_count, BLOCK, width)
    local_part = jnp.einsum("dts,nsd->ntd", toeplitz, blocked, preferred_element_type=jnp.float32)
    blocked_wide = blocked.astype(jnp.float32)
    end_weight = jnp.exp(-(BLOCK - 1 - position)[:, None, None] * rate_modes[None])
    block_ends = jnp.einsum(
        "tkd,ntd->nkd", end_weight, blocked_wide, precision=lax.Precision.HIGHEST
    )
    step_decay = jnp.exp(-BLOCK * rate_modes)

    def advance(carry_state, inflow):
        return (step_decay * carry_state + inflow, carry_state)

    end_state, starts_local = lax.scan(advance, jnp.zeros((ORDER, width), jnp.float32), block_ends)
    shard_decay = jnp.exp(-tok_rows * rate_modes)

    def combine_pairs(earlier, later):
        return (earlier[0] * later[0], earlier[1] * later[0] + later[1])

    identity = (jnp.ones_like(shard_decay), jnp.zeros_like(end_state))
    scanned = entering((shard_decay, end_state), "seq", combine_pairs, identity)
    incoming = scanned[1]
    block_index = jnp.arange(block_count, dtype=jnp.float32)
    starts = (
        starts_local
        + jnp.exp(-(BLOCK * block_index)[:, None, None] * rate_modes[None]) * incoming[None]
    )
    reach_table = mode_coef[None] * jnp.exp(-(position + 1.0)[:, None, None] * rate_modes[None])
    correction = jnp.einsum("tkd,nkd->ntd", reach_table, starts, precision=lax.Precision.HIGHEST)
    conv = (local_part + correction).reshape(tok_rows, width)
    gated = (
        q_gate.astype(jnp.float32) * (conv + skip_gain[None] * values_in.astype(jnp.float32))
    ).astype(jnp.bfloat16)
    weights = lax.all_gather(out_weight, "seq", axis=0, tiled=True)
    mixed = jnp.dot(gated, weights, preferred_element_type=jnp.float32)
    return mixed.astype(jnp.bfloat16)


def solution(mesh):
    in_specs = (
        P(("groups", "seq"), None),
        P(("groups", "seq"), None),
        P(),
        P(),
        P(),
        P("seq", None),
    )
    out_specs = P(("groups", "seq"), None)
    return jax.shard_map(
        on_device, mesh=mesh, in_specs=in_specs, out_specs=out_specs, check_vma=False
    )
```

profile of v0, /device:TPU:0, one launch (start us, length us, event | category | flops | bytes accessed | tf_op | source)
XLA Modules:
  0.0 299.8 jit_solution(8403443552745695005)
XLA Ops:
  6.5 1.9 multiply_exponential_fusion
  8.5 0.0 all-gather.8.cloned.1.call-update
  8.5 0.0 all-gather.10.cloned.1.call-start
  8.6 1.5 copy.31
  10.1 6.2 %copy.34 = bf16[4,32,4096]{1,0,2:T(4,128)(2,1)} copy(bf16[4,32,4096]{2,1,0:T(8,128)(2,1)} %bitcast.53) | data formatting | bytes 2097152 | tf_op jit(solution)/shard_map/reshape | solution.py:45
  16.3 34.1 %fusion.13 = f32[4,16,4096]{1,0,2:T(4,128)} fusion(bf16[4,32,4096]{1,0,2:T(4,128)(2,1)} %copy.34, f32[32]{0:T(128)S(1)} %subtract_negate_fusion, f32[16,4096]{0,1:T(8,128)S(1)} %copy.31), kind=kOutput, calls=%fused_computation.19 | convolution fusion | flops 102760448 | bytes 2359424 | tf_op jit(solution)/shard_map/tkd,ntd->nkd/dot_general | solution.py:49
  50.4 7.5 %copy.36 = f32[4,16,4096]{2,1,0:T(8,128)} copy(f32[4,16,4096]{1,0,2:T(4,128)} %fusion.13) | data formatting | bytes 2097152
  57.9 7.5 %while.27 = (s32[]{:T(128)}, f32[16,4096]{1,0:T(8,128)S(1)}, f32[4,16,4096]{2,1,0:T(8,128)}, f32[16,4096]{1,0:T(8,128)S(1)}, f32[4,16,4096]{2,1,0:T(8,128)}, /*index=5*/s32[]{:T(128)}, s32[]{:T(128)}) while((s32[]{:T(128)}, f32[16,4096]{1,0:T(8,128)S(1)}, f32[4,16,4096]{2,1,0:T(8,128)}, f32[16,4096]{1,0:T(8,128)S(1)}, ...), condition=%wide.region_2.3_spmd.clone, body=%wide.region_1.2_spmd.clone.sunk | while | flops 262147 | bytes 1572968 | solution.py:57
  57.9 0.7 bitcast_dynamic-update-slice_fusion.2
  58.7 1.1 bitcast_add_fusion.5
  59.8 0.7 bitcast_dynamic-update-slice_fusion.2
  60.5 1.2 bitcast_add_fusion.5
  61.7 0.7 bitcast_dynamic-update-slice_fusion.2
  62.5 1.1 bitcast_add_fusion.5
  63.6 0.7 bitcast_dynamic-update-slice_fusion.2
  64.3 1.1 bitcast_add_fusion.5
  65.4 0.7 copy-done
  66.2 0.2 all-gather.6.cloned.1.call-start
  66.4 0.5 all-gather.6.cloned.1.call-update
  67.0 2.0 copy.30
  68.9 25.7 %multiply_reduce_fusion = bf16[32,4096]{0,1:T(8,128)(2,1)} fusion(f32[16,4096]{0,1:T(8,128)S(1)} %copy.31, f32[32]{0:T(128)S(1)} %iota_negate_fusion, f32[16,4096]{0,1:T(8,128)} %copy.30), kind=kLoop, calls=%fused_computation.12 | loop fusion | flops 6160384 | bytes 786560 | tf_op jit(solution)/shard_map/reduce_sum | solution.py:32
  94.6 1.5 copy.32
  96.2 5.6 %fusion.20 = bf16[4096,32,32]{0,2,1:T(8,128)(2,1)} fusion(s32[32,32]{1,0:T(8,128)S(1)} %iota_subtract_fusion, bf16[32,4096]{1,0:T(8,128)(2,1)S(1)} %copy.32), kind=kOutput, calls=%fused_computation.26 | convolution fusion | flops 268468224 | bytes 8654848 | tf_op jit(solution)/shard_map/dot_general | solution.py:42
  101.7 44.1 %copy.33 = bf16[4096,32,32]{2,1,0:T(8,128)(2,1)} copy(bf16[4096,32,32]{0,2,1:T(8,128)(2,1)} %fusion.20) | data formatting | bytes 16777216 | tf_op jit(solution)/shard_map/dot_general | solution.py:42
  145.9 22.9 %fusion.24 = f32[4096,32,4]{1,2,0:T(4,128)} fusion(bf16[4096,32,32]{2,1,0:T(8,128)(2,1)} %copy.33, bf16[4,32,4096]{1,0,2:T(4,128)(2,1)} %copy.34), kind=kOutput, calls=%fused_computation.38 | convolution fusion | flops 33554432 | bytes 11534336 | tf_op jit(solution)/shard_map/dts,nsd->ntd/dot_general | solution.py:46
  168.8 39.5 %while.28 = (s32[]{:T(128)}, f32[16,4096]{1,0:T(8,128)S(1)}, s32[]{:T(128)}, f32[32,16,4096]{2,1,0:T(8,128)}, f32[32,16,4096]{2,1,0:T(8,128)}, /*index=5*/s32[]{:T(128)}, s32[]{:T(128)}) while((s32[]{:T(128)}, f32[16,4096]{1,0:T(8,128)S(1)}, s32[]{:T(128)}, f32[32,16,4096]{2,1,0:T(8,128)}, f32[32,16,4096]{2,1,0:T(8,128)}, ...), condition=%wide.region_4.5_spmd.clone, body=%wide.region_3.4_spmd.clone.sunk | while | flops 262148 | bytes 1048685 | solution.py:21
  168.8 1.2 fusion.35
  170.0 1.2 fusion.35
  171.3 1.2 fusion.35
  172.6 1.2 fusion.35
  173.9 1.2 fusion.35
  175.1 1.2 fusion.35
  176.4 1.2 fusion.35
  177.7 1.3 fusion.35
  179.0 1.3 fusion.35
  180.3 1.2 fusion.35
  181.6 1.2 fusion.35
  182.8 1.2 fusion.35
  184.1 1.3 fusion.35
  185.4 1.3 fusion.35
  186.7 1.2 fusion.35
  187.9 1.2 fusion.35
  189.2 1.2 fusion.35
  190.5 1.3 fusion.35
  191.8 1.2 fusion.35
  193.0 1.2 fusion.35
  194.3 1.2 fusion.35
  195.6 1.2 fusion.35
  196.8 1.2 fusion.35
  198.1 1.2 fusion.35
  199.4 1.3 fusion.35
  200.7 1.2 fusion.35
  202.0 1.2 fusion.35
  203.2 1.2 fusion.35
  204.5 1.3 fusion.35
  205.8 1.2 fusion.35
  207.1 1.3 fusion.35
  208.3 2.5 multiply_add_fusion
  210.9 6.9 %copy.37 = f32[4,16,4096]{1,0,2:T(4,128)} copy(f32[4,16,4096]{2,1,0:T(8,128)} %multiply_add_fusion) | data formatting | bytes 2097152 | tf_op jit(solution)/shard_map/add | solution.py:68
  217.7 47.3 %bitcast_add_fusion.2 = f32[4,32,4096]{1,0,2:T(4,128)} fusion(f32[4096,32,4]{1,2,0:T(4,128)} %fusion.24, f32[4,16,4096]{1,0,2:T(4,128)} %copy.37, f32[32]{0:T(128)S(1)} %add_negate_fusion, f32[16,4096]{0,1:T(8,128)S(1)} %copy.31, f32[16,4096]{0,1:T(8,128)} %copy.30), kind=kOutput, calls=%fused_computation.18 | convolution fusion | flops 105381888 | bytes 5767296 | tf_op jit(solution)/shard_map/tkd,nkd->ntd/dot_general | solution.py:72
  265.1 7.0 %copy.38 = f32[4,32,4096]{2,1,0:T(8,128)S(1)} copy(f32[4,32,4096]{1,0,2:T(4,128)} %bitcast_add_fusion.2) | data formatting | bytes 4194304 | tf_op jit(solution)/shard_map/add | solution.py:73
  272.1 2.2 fusion.19
  274.3 10.2 %all-gather.6.cloned.1.call-done = bf16[4096,2048]{1,0:T(8,128)(2,1)} async-done(((bf16[128,2048]{1,0:T(8,128)(2,1)}), bf16[4096,2048]{1,0:T(8,128)(2,1)}) %all-gather.6.cloned.1.call-update) | async-done | bytes 16777232 | tf_op jit(solution)/shard_map/all_gather | solution.py:77
  284.4 8.9 %convolution_convert_fusion = bf16[128,2048]{1,0:T(8,128)(2,1)} fusion(bf16[128,4096]{1,0:T(8,128)(2,1)S(1)} %fusion.19, bf16[4096,2048]{1,0:T(8,128)(2,1)} %all-gather.6.cloned.1.call-done), kind=kOutput, calls=%fused_computation.20 | convolution fusion | flops 2147745792 | bytes 18350080 | tf_op jit(solution)/shard_map/dot_general | solution.py:78
  (17 shorter events, 0.1 us)
Async XLA Ops:
  6.5 162.2 %all-gather.8.cloned.1.call-start = ((), (), s32[]{:S(2)}) async-start(), calls=%async_computation.1 | async-start | bytes 8650752 | tf_op jit(solution)/shard_map/all_gather | solution.py:12
  8.5 160.3 %all-gather.10.cloned.1.call-start = ((), (), s32[]{:S(2)}) async-start(), calls=%async_computation.2 | async-start | bytes 8650752 | tf_op jit(solution)/shard_map/all_gather | solution.py:12
  65.4 0.7 copy-start
  66.2 218.3 %all-gather.6.cloned.1.call-start = ((), (), s32[]{:S(2)}) async-start(), calls=%async_computation | async-start | bytes 17301504 | tf_op jit(solution)/shard_map/all_gather | solution.py:77
  145.9 62.4 %copy-start.1 = (f32[4096,16]{0,1:T(8,128)S(1)}, f32[4096,16]{0,1:T(8,128)}, u32[]{:S(2)}) copy-start(f32[4096,16]{0,1:T(8,128)} %param.12) | copy-start | bytes 786436
  265.1 7.0 %copy-start.2 = (f32[4096]{0:T(1024)S(1)}, f32[4096]{0:T(1024)}, u32[]{:S(2)}) copy-start(f32[4096]{0:T(1024)} %param.14) | copy-start | bytes 49156
Sparse Core Ops, SparseCore 0:
  10.2 79.7 all-gather.7
  92.9 75.6 all-gather.9
  171.4 112.9 all-gather.5
where the time goes:
time: 302 us; the launch traced here: 300 us
  matrix products  119 us (39%)
  other arithmetic  78.6 us (26%)
  local copies, waits for them, and re-layouts  77.5 us (26%)
  between operations  13.2 us (4%)
  waiting for transfers between devices  10.7 us (4%)
    dot_general x1, matrix products, on_device(): jnp.einsum('tkd,nkd->ntd', reach_table, starts, precision=lax.Precision.H...  47.3 us
    dot_general x1, local copies, waits for them, and re-layouts, on_device(): jnp.dot(tap_round.T, selector, preferred_element_type=jnp.bfloat16)  44.1 us
    select_n x31, other arithmetic, hop(): jnp.where(position < mine, new, old)  38.9 us
    dot_general x1, matrix products, on_device(): jnp.einsum('tkd,ntd->nkd', end_weight, blocked_wide, precision=lax.Precis...  34.1 us
    reduce_sum x1, other arithmetic, on_device(): jnp.sum(mode_coef[None] * jnp.exp(-position[:, None, None] * rate_modes[N...  25.7 us
    dot_general x1, matrix products, on_device(): jnp.einsum('dts,nsd->ntd', toeplitz, blocked, preferred_element_type=jnp....  22.9 us
    all_gather x1, waiting for transfers between devices, on_device(): weights = lax.all_gather(out_weight, 'seq', axis=0, tiled=True)  10.2 us
    dot_general x1, matrix products, on_device(): mixed = jnp.dot(gated, weights, preferred_element_type=jnp.float32)  8.9 us
  transfers between devices with their start and end apart: 3, of which 1 were waited for; matrix products, arithmetic and copies ran while one was open for 88% of the time, Pallas kernels for 0%

commit v1 on v0

v1 whole, which is shorter than its diff:
```python
import functools

import jax
import jax.numpy as jnp
from jax import lax
from jax.experimental import pallas as pl
from jax.experimental.pallas import tpu as pltpu
from jax.sharding import PartitionSpec as P

ORDER = 16
BLOCK = 32
SUB = 8
LANES = 128
PARTS = BLOCK // SUB


def row(ref, at, lanes):
    return jnp.broadcast_to(ref[pl.ds(at, 1), lanes], (SUB, LANES))


def local_kernel(tok_rows, width, v_ref, rate_ref, res_ref, conv_ref, ends_ref, last_ref, pad, taps, mult):
    blocks = tok_rows // BLOCK
    zero = jnp.zeros((SUB, LANES), jnp.float32)
    steps = lax.broadcasted_iota(jnp.int32, (SUB, LANES), 0).astype(jnp.float32)

    def group(g, carry):
        lanes = pl.ds(pl.multiple_of(g * LANES, LANES), LANES)
        rate = rate_ref[:, lanes]
        lam = jnp.exp(-rate)
        coef = res_ref[:, lanes]
        for n in range(blocks):
            pad[n, 0:SUB, :] = zero
            pad[n, SUB : SUB + BLOCK, :] = v_ref[n * BLOCK : (n + 1) * BLOCK, lanes].astype(jnp.float32)
        for part in range(PARTS):
            mult[part * ORDER : (part + 1) * ORDER, :] = coef * jnp.exp(-float(SUB * part) * rate)
        sums = [zero] * PARTS
        for k in range(ORDER):
            base = jnp.exp(-steps * jnp.broadcast_to(rate[k : k + 1], (SUB, LANES)))
            for part in range(PARTS):
                at = part * ORDER + k
                sums[part] += base * jnp.broadcast_to(mult[at : at + 1, :], (SUB, LANES))
        for part in range(PARTS):
            taps[part * SUB : (part + 1) * SUB, :] = sums[part].astype(jnp.bfloat16).astype(jnp.float32)
        for n in range(blocks):
            acc = [zero] * PARTS
            for r in range(SUB):
                shifted = [
                    pad[n, SUB - r + SUB * i : 2 * SUB - r + SUB * i, :] for i in range(PARTS)
                ]
                for part in range(PARTS):
                    at = part * SUB + r
                    tap = jnp.broadcast_to(taps[at : at + 1, :], (SUB, LANES))
                    for i in range(part, PARTS):
                        acc[i] += tap * shifted[i - part]
            for i in range(PARTS):
                conv_ref[n * BLOCK + SUB * i : n * BLOCK + SUB * (i + 1), lanes] = acc[i]
        ends = [jnp.zeros((ORDER, LANES), jnp.float32)] * blocks
        for t in range(BLOCK):
            for n in range(blocks):
                ends[n] = lam * ends[n] + jnp.broadcast_to(pad[n, SUB + t : SUB + t + 1, :], (ORDER, LANES))
        step_decay = jnp.exp(-float(BLOCK) * rate)
        state = jnp.zeros((ORDER, LANES), jnp.float32)
        for n in range(blocks):
            ends_ref[n * ORDER : (n + 1) * ORDER, lanes] = state
            state = step_decay * state + ends[n]
        last_ref[:, lanes] = state
        return carry

    lax.fori_loop(0, width // LANES, group, 0)


def gate_kernel(tok_rows, width, q_ref, v_ref, conv_ref, ends_ref, in_ref, rate_ref, res_ref, skip_ref, out_ref, mult, whole):
    blocks = tok_rows // BLOCK
    zero = jnp.zeros((SUB, LANES), jnp.float32)
    steps = lax.broadcasted_iota(jnp.int32, (SUB, LANES), 0).astype(jnp.float32) + 1.0

    def group(g, carry):
        lanes = pl.ds(pl.multiple_of(g * LANES, LANES), LANES)
        rate = rate_ref[:, lanes]
        coef = res_ref[:, lanes]
        entering = in_ref[:, lanes]
        for n in range(blocks):
            state = ends_ref[n * ORDER : (n + 1) * ORDER, lanes] + jnp.exp(-float(BLOCK * n) * rate) * entering
            state = coef * state
            for part in range(PARTS):
                at = (n * PARTS + part) * ORDER
                mult[at : at + ORDER, :] = state * jnp.exp(-float(SUB * part) * rate)
        for k in range(ORDER):
            whole[k] = jnp.exp(-steps * jnp.broadcast_to(rate[k : k + 1], (SUB, LANES)))
        skip = jnp.broadcast_to(skip_ref[:, lanes], (BLOCK, LANES))
        for n in range(blocks):
            acc = [zero] * PARTS
            for k in range(ORDER):
                base = whole[k]
                for part in range(PARTS):
                    at = (n * PARTS + part) * ORDER + k
                    acc[part] += base * jnp.broadcast_to(mult[at : at + 1, :], (SUB, LANES))
            rows = pl.ds(n * BLOCK, BLOCK)
            conv = conv_ref[rows, lanes] + jnp.concatenate(acc, axis=0)
            value = v_ref[rows, lanes].astype(jnp.float32)
            gated = q_ref[rows, lanes].astype(jnp.float32) * (conv + skip * value)
            out_ref[rows, lanes] = gated.astype(jnp.bfloat16)
        return carry

    lax.fori_loop(0, width // LANES, group, 0)


def scan_kernel(count, tok_rows, in_ref, rate_ref, out_ref):
    decay = jnp.exp(-float(tok_rows) * rate_ref[...])

    def hop(i, state):
        out_ref[i] = state
        return decay * state + in_ref[i]

    lax.fori_loop(0, count, hop, jnp.zeros_like(decay))


def on_device(q_gate, values_in, decay_rate, residue, skip_gain, out_weight):
    tok_rows, width = q_gate.shape
    out_width = out_weight.shape[1]
    half = out_width // 2
    count = lax.axis_size("seq")
    me = lax.axis_index("seq")
    core = me % 2
    swap = [(i, i ^ 1) for i in range(count)]

    keep = lax.dynamic_slice_in_dim(out_weight, core * half, half, 1)
    give = lax.dynamic_slice_in_dim(out_weight, (1 - core) * half, half, 1)
    take = lax.ppermute(give, "seq", swap)
    pair = jnp.where(core == 0, jnp.concatenate([keep, take]), jnp.concatenate([take, keep]))
    sides = [list(range(0, count, 2)), list(range(1, count, 2))]
    weights = lax.all_gather(pair, "seq", axis=0, tiled=True, axis_index_groups=sides)

    rate = decay_rate.T
    coef = residue.T * jnp.sqrt(-jnp.expm1(-2.0 * rate))
    chunk = 1024
    blocks = tok_rows // BLOCK
    grid = (width // chunk,)
    tall = lambda rows: pl.BlockSpec((rows, chunk), lambda c: (0, c))
    conv, starts, last = pl.pallas_call(
        functools.partial(local_kernel, tok_rows, chunk),
        grid=grid,
        in_specs=[tall(tok_rows), tall(ORDER), tall(ORDER)],
        out_specs=[tall(tok_rows), tall(blocks * ORDER), tall(ORDER)],
        out_shape=[
            jax.ShapeDtypeStruct((tok_rows, width), jnp.float32),
            jax.ShapeDtypeStruct((blocks * ORDER, width), jnp.float32),
            jax.ShapeDtypeStruct((ORDER, width), jnp.float32),
        ],
        scratch_shapes=[
            pltpu.VMEM((blocks, SUB + BLOCK, LANES), jnp.float32),
            pltpu.VMEM((BLOCK, LANES), jnp.float32),
            pltpu.VMEM((PARTS * ORDER, LANES), jnp.float32),
        ],
        name="local_conv",
    )(values_in, rate, coef)

    own = width // count
    spread = last.reshape(ORDER, count, own).transpose(1, 0, 2)
    owned = lax.all_to_all(spread, "seq", 0, 0, tiled=True)
    rate_own = lax.dynamic_slice_in_dim(rate, me * own, own, 1)
    scanned = pl.pallas_call(
        functools.partial(scan_kernel, count, tok_rows),
        out_shape=jax.ShapeDtypeStruct((count, ORDER, own), jnp.float32),
        name="state_scan",
    )(owned, rate_own)
    back = lax.all_to_all(scanned, "seq", 0, 0, tiled=True)
    entering = back.transpose(1, 0, 2).reshape(ORDER, width)

    gated = pl.pallas_call(
        functools.partial(gate_kernel, tok_rows, chunk),
        grid=grid,
        in_specs=[tall(tok_rows), tall(tok_rows), tall(tok_rows), tall(blocks * ORDER), tall(ORDER), tall(ORDER), tall(ORDER), tall(1)],
        out_specs=tall(tok_rows),
        out_shape=jax.ShapeDtypeStruct((tok_rows, width), jnp.bfloat16),
        scratch_shapes=[
            pltpu.VMEM((blocks * PARTS * ORDER, LANES), jnp.float32),
            pltpu.VMEM((ORDER, SUB, LANES), jnp.float32),
        ],
        name="gate",
    )(q_gate, values_in, conv, starts, entering, rate, coef, skip_gain[None])

    other = lax.ppermute(gated, "seq", swap)
    both = jnp.concatenate([gated, other])
    mixed = jnp.dot(both, weights, preferred_element_type=jnp.float32).astype(jnp.bfloat16)
    mine = mixed[:tok_rows]
    far = lax.ppermute(mixed[tok_rows:], "seq", swap)
    return jnp.where(core == 0, jnp.concatenate([mine, far], 1), jnp.concatenate([far, mine], 1))


def solution(mesh):
    in_specs = (
        P(("groups", "seq"), None),
        P(("groups", "seq"), None),
        P(),
        P(),
        P(),
        P("seq", None),
    )
    out_specs = P(("groups", "seq"), None)
    return jax.shard_map(
        on_device, mesh=mesh, in_specs=in_specs, out_specs=out_specs, check_vma=False
    )
```

time: 302 us -> 150 us (0.50)
  matrix products: 119 us -> 6.04 us
  other arithmetic: 78.6 us -> 3.76 us
  local copies, waits for them, and re-layouts: 77.5 us -> 5.53 us
  waiting for transfers between devices: 10.7 us -> 76.3 us
  blocking collectives: 0 us -> 19.4 us
  Pallas kernels: 0 us -> 17 us
  starting transfers between devices: 0.27 us -> 8.03 us
    dot_general x5 -> x1, matrix products: 119 us -> 6.04 us  [on_device(): jnp.dot(both, weights, preferred_element_type=jnp.float32)]
    all_gather x3 -> x1, waiting for transfers between devices: 10.2 us -> 58.4 us  [on_device(): lax.all_gather(pair, 'seq', axis=0, tiled=True, axis_index_groups=sides)]
    dot_general x1 -> x0, local copies, waits for them, and re-layouts: 44.1 us -> none  [on_device(): jnp.dot(tap_round.T, selector, preferred_element_type=jnp.bfloat16)]
    select_n x31 -> x2, other arithmetic: 38.9 us -> 1.85 us  [the longest x1 0.93 us: on_device(): jnp.where(core == 0, jnp.concatenate([keep, take]), jnp.concatenate([take...]
    reduce_sum x1 -> x0, other arithmetic: 25.7 us -> none  [on_device(): jnp.sum(mode_coef[None] * jnp.exp(-position[:, None, None] * rate_modes[N...]
    all_to_all x0 -> x1, blocking collectives: none -> 19.4 us  [on_device(): back = lax.all_to_all(scanned, 'seq', 0, 0, tiled=True)]
    pallas_call x0 -> x3, Pallas kernels: none -> 17 us  [the longest x1 8.87 us: on_device(): pl.pallas_call(functools.partial(local_kernel, tok_rows, chunk), grid=gri...]
    add x2 -> x0, local copies, waits for them, and re-layouts: 13.9 us -> none  [the longest x1 7.02 us: on_device(): conv = (local_part + correction).reshape(tok_rows, width)]
  transfers between devices with their start and end apart: 3 -> 5, of which waited for: 1 -> 5; matrix products, arithmetic and copies ran while one was open for 88% -> 4% of each run, Pallas kernels for 0% -> 11%
where the time goes in v1:
time: 150 us; the launch traced here: 149 us
  waiting for transfers between devices  76.3 us (51%)
  blocking collectives  19.4 us (13%)
  Pallas kernels  17 us (11%)
  between operations  13.4 us (9%)
  starting transfers between devices  8.03 us (5%)
  matrix products  6.04 us (4%)
  local copies, waits for them, and re-layouts  5.53 us (4%)
  other arithmetic  3.76 us (3%)
    all_gather x1, waiting for transfers between devices, on_device(): lax.all_gather(pair, 'seq', axis=0, tiled=True, axis_index_groups=sides)  58.4 us
    all_to_all x1, blocking collectives, on_device(): back = lax.all_to_all(scanned, 'seq', 0, 0, tiled=True)  19.4 us
    all_to_all x1, waiting for transfers between devices, on_device(): owned = lax.all_to_all(spread, 'seq', 0, 0, tiled=True)  12.5 us
    pallas_call x1, Pallas kernels, on_device(): pl.pallas_call(functools.partial(local_kernel, tok_rows, chunk), grid=gri...  8.87 us
    all_to_all x1, starting transfers between devices, on_device(): owned = lax.all_to_all(spread, 'seq', 0, 0, tiled=True)  7.2 us
    pallas_call x1, Pallas kernels, on_device(): pl.pallas_call(functools.partial(gate_kernel, tok_rows, chunk), grid=grid...  6.25 us
    dot_general x1, matrix products, on_device(): jnp.dot(both, weights, preferred_element_type=jnp.float32)  6.04 us
  transfers between devices with their start and end apart: 5, of which 5 were waited for; matrix products, arithmetic and copies ran while one was open for 4% of the time, Pallas kernels for 11%

profile of v1, /device:TPU:0, one launch (start us, length us, event | category | flops | bytes accessed | tf_op | source)
XLA Modules:
  0.0 149.5 jit_solution(5097531033832029785)
XLA Ops:
  6.5 0.0 all-gather.2.cloned.1.call-start
  6.5 1.1 constant_dynamic-slice_fusion.1
  7.6 0.6 collective-permute-start.1
  8.2 1.2 collective-permute-done.1
  9.3 0.9 maximum_select_fusion
  10.3 0.0 all-gather.2.cloned.1.call-update
  10.3 1.9 %bitcast_multiply_fusion.res_ref = f32[16,4096]{1,0:T(8,128)} fusion(f32[4096,16]{0,1:T(8,128)} %param.9, f32[4096,16]{0,1:T(8,128)} %param.8), kind=kLoop, calls=%fused_computation.9 | loop fusion | flops 196608 | bytes 786432 | tf_op jit(solution)/shard_map/mul | solution.py:135
  12.2 8.9 %local_conv.1 = (f32[128,4096]{1,0:T(8,128)}, f32[64,4096]{1,0:T(8,128)}, f32[16,4096]{1,0:T(8,128)}) custom-call(bf16[128,4096]{1,0:T(8,128)(2,1)} %v_ref.3, f32[16,4096]{1,0:T(8,128)} %bitcast.21, f32[16,4096]{1,0:T(8,128)} %bitcast_multiply_fusion.res_ref), custom_call_target="tpu_custom_call" | custom-call | tf_op jit(solution)/shard_map/local_conv/pallas_call | solution.py:140
  21.1 1.7 %bitcast_bitcast_fusion = f32[32,16,128]{2,1,0:T(8,128)} fusion(f32[16,4096]{1,0:T(8,128)} %get-tuple-element.10), kind=kLoop, calls=%fused_computation.8 | loop fusion | bytes 524288 | tf_op jit(solution)/shard_map/transpose | solution.py:159
  22.8 7.2 %all-to-all-start = ((f32[32,16,128]{2,1,0:T(8,128)}), f32[32,16,128]{2,1,0:T(8,128)S(1)}, u32[]{:S(2)}, u32[]{:S(2)}) async-start(f32[32,16,128]{2,1,0:T(8,128)} %bitcast_bitcast_fusion), calls=%async_computation | async-start | bytes 524288 | tf_op jit(solution)/shard_map/all_to_all | solution.py:160
  30.0 1.3 dynamic-slice_bitcast_fusion.rate_ref
  31.3 12.5 %all-to-all-done.in_ref = f32[32,16,128]{2,1,0:T(8,128)S(1)} async-done(((f32[32,16,128]{2,1,0:T(8,128)}), f32[32,16,128]{2,1,0:T(8,128)S(1)}, u32[]{:S(2)}, u32[]{:S(2)}) %all-to-all-start) | async-done | bytes 262176 | tf_op jit(solution)/shard_map/all_to_all | solution.py:160
  43.8 0.0 copy-start
  43.8 0.7 copy-done
  44.5 1.8 %state_scan.1 = f32[32,16,128]{2,1,0:T(8,128)} custom-call(f32[32,16,128]{2,1,0:T(8,128)} %copy-done, f32[16,128]{1,0:T(8,128)} %dynamic-slice_bitcast_fusion.rate_ref), custom_call_target="tpu_custom_call" | custom-call | tf_op jit(solution)/shard_map/state_scan/pallas_call | solution.py:162
  46.3 19.4 %all_to_all.10 = f32[32,16,128]{2,1,0:T(8,128)S(1)} all-to-all(f32[32,16,128]{2,1,0:T(8,128)} %state_scan.1), channel_id=1, replica_groups=mesh['groups'=1,'seq'=32] {'seq'}, dimensions={0} | all-to-all | bytes 524288 | tf_op jit(solution)/shard_map/all_to_all | solution.py:167
  65.8 0.7 copy_bitcast_fusion.in_ref
  66.5 6.3 %gate.1 = bf16[128,4096]{1,0:T(8,128)(2,1)} custom-call(bf16[128,4096]{1,0:T(8,128)(2,1)} %q_ref.1, bf16[128,4096]{1,0:T(8,128)(2,1)} %v_ref.3, f32[128,4096]{1,0:T(8,128)} %get-tuple-element.8.conv_ref, f32[64,4096]{1,0:T(8,128)} %get-tuple-element.9.ends_ref, f32[16,4096]{1,0:T(8,128)} %copy_bitcast_fusion.in_ref, f32[16,4096]{1,0:T(8,128)} %bitcast.22, ...), custom_call_target="tpu_custom_call" | custom-call | tf_op jit(solution)/shard_map/gate/pallas_call | solution.py:170
  72.8 0.2 collective-permute-start
  73.0 2.7 %collective-permute-done = bf16[128,4096]{1,0:T(8,128)(2,1)S(1)} collective-permute-done((bf16[128,4096]{1,0:T(8,128)(2,1)}, bf16[128,4096]{1,0:T(8,128)(2,1)S(1)}, u32[]{:S(2)}, u32[]{:S(2)}) %collective-permute-start) | collective-permute-done | bytes 1048608 | tf_op jit(solution)/shard_map/ppermute | solution.py:183
  75.6 58.4 %all-gather.2.cloned.1.call-done = bf16[4096,1024]{1,0:T(8,128)(2,1)} async-done(((bf16[256,1024]{1,0:T(8,128)(2,1)}), bf16[4096,1024]{1,0:T(8,128)(2,1)}) %all-gather.2.cloned.1.call-update) | async-done | bytes 8388624 | tf_op jit(solution)/shard_map/all_gather | solution.py:132
  134.0 6.0 %fusion.4 = bf16[256,1024]{1,0:T(8,128)(2,1)S(1)} fusion(bf16[4096,1024]{1,0:T(8,128)(2,1)} %all-gather.2.cloned.1.call-done, bf16[128,4096]{1,0:T(8,128)(2,1)S(1)} %collective-permute-done, bf16[128,4096]{1,0:T(8,128)(2,1)} %gate.1), kind=kOutput, calls=%fused_computation.4 | convolution fusion | flops 2151940096 | bytes 11010048 | tf_op jit(solution)/shard_map/dot_general | solution.py:185
  140.1 0.1 collective-permute-start.2
  140.2 1.5 %collective-permute-done.2 = bf16[128,1024]{1,0:T(8,128)(2,1)S(1)} collective-permute-done((bf16[128,1024]{1,0:T(8,128)(2,1)S(1)}, bf16[128,1024]{1,0:T(8,128)(2,1)S(1)}, u32[]{:S(2)}, u32[]{:S(2)}) %collective-permute-start.2) | collective-permute-done | bytes 262176 | tf_op jit(solution)/shard_map/ppermute | solution.py:187
  141.7 0.9 maximum_select_fusion.1
  (1 shorter events, 0.0 us)
Async XLA Ops:
  6.5 127.5 %all-gather.2.cloned.1.call-start = ((), (), s32[]{:S(2)}) async-start(), calls=%async_computation.2 | async-start | bytes 8912896 | tf_op jit(solution)/shard_map/all_gather | solution.py:132
  7.6 1.7 %collective-permute-start.1 = (bf16[128,1024]{1,0:T(8,128)(2,1)S(1)}, bf16[128,1024]{1,0:T(8,128)(2,1)S(1)}, u32[]{:S(2)}, u32[]{:S(2)}) collective-permute-start(bf16[128,1024]{1,0:T(8,128)(2,1)S(1)} %get-tuple-element.14), channel_id=1, source_target_pairs={{0,1},{1,0},{2,3},{3,2},{4,5},{5,4},{6,7},{7,6},{8,9},{9,8},{10,11... | collective-permute-start | bytes 786440 | tf_op jit(solution)/shard_map/ppermute | solution.py:129
  22.8 21.1 %all-to-all-start = ((f32[32,16,128]{2,1,0:T(8,128)}), f32[32,16,128]{2,1,0:T(8,128)S(1)}, u32[]{:S(2)}, u32[]{:S(2)}) async-start(f32[32,16,128]{2,1,0:T(8,128)} %bitcast_bitcast_fusion), calls=%async_computation | async-start | bytes 524288 | tf_op jit(solution)/shard_map/all_to_all | solution.py:160
  43.8 0.7 copy-start
  72.8 2.9 %collective-permute-start = (bf16[128,4096]{1,0:T(8,128)(2,1)}, bf16[128,4096]{1,0:T(8,128)(2,1)S(1)}, u32[]{:S(2)}, u32[]{:S(2)}) collective-permute-start(bf16[128,4096]{1,0:T(8,128)(2,1)} %gate.1), channel_id=1, source_target_pairs={{0,1},{1,0},{2,3},{3,2},{4,5},{5,4},{6,7},{7,6},{8,9},{9,8},{10,11... | collective-permute-start | bytes 3145736 | tf_op jit(solution)/shard_map/ppermute | solution.py:183
  140.1 1.6 %collective-permute-start.2 = (bf16[128,1024]{1,0:T(8,128)(2,1)S(1)}, bf16[128,1024]{1,0:T(8,128)(2,1)S(1)}, u32[]{:S(2)}, u32[]{:S(2)}) collective-permute-start(bf16[128,1024]{1,0:T(8,128)(2,1)S(1)} %get-tuple-element.12), channel_id=1, source_target_pairs={{0,1},{1,0},{2,3},{3,2},{4,5},{5,4},{6,7},{7,6},{8,9},{9,8},{10,11... | collective-permute-start | bytes 786440 | tf_op jit(solution)/shard_map/ppermute | solution.py:187
Sparse Core Ops, SparseCore 0:
  10.4 123.5 all-gather.1

commit v2 on v1

--- a/solution.py
+++ b/solution.py
@@ -1,4 +1,5 @@
 import functools
+import math
 
 import jax
 import jax.numpy as jnp
@@ -12,13 +13,15 @@
 SUB = 8
 LANES = 128
 PARTS = BLOCK // SUB
+GRID = (4, 2, 2)
+MESH = pl.DeviceIdType.MESH
 
 
 def row(ref, at, lanes):
     return jnp.broadcast_to(ref[pl.ds(at, 1), lanes], (SUB, LANES))
 
 
-def local_kernel(tok_rows, width, v_ref, rate_ref, res_ref, conv_ref, ends_ref, last_ref, pad, taps, mult):
+def local_group(tok_rows, v_ref, rate_ref, res_ref, conv_ref, ends_ref, put_last, pad, taps, mult):
     blocks = tok_rows // BLOCK
     zero = jnp.zeros((SUB, LANES), jnp.float32)
     steps = lax.broadcasted_iota(jnp.int32, (SUB, LANES), 0).astype(jnp.float32)
@@ -63,13 +66,21 @@
         for n in range(blocks):
             ends_ref[n * ORDER : (n + 1) * ORDER, lanes] = state
             state = step_decay * state + ends[n]
+        put_last(g, lanes, state)
+        return carry
+
+    return group
+
+
+def local_kernel(tok_rows, width, v_ref, rate_ref, res_ref, conv_ref, ends_ref, last_ref, pad, taps, mult):
+    def put_last(g, lanes, state):
         last_ref[:, lanes] = state
-        return carry
-
+
+    group = local_group(tok_rows, v_ref, rate_ref, res_ref, conv_ref, ends_ref, put_last, pad, taps, mult)
     lax.fori_loop(0, width // LANES, group, 0)
 
 
-def gate_kernel(tok_rows, width, q_ref, v_ref, conv_ref, ends_ref, in_ref, rate_ref, res_ref, skip_ref, out_ref, mult, whole):
+def gate_group(tok_rows, q_ref, v_ref, conv_ref, ends_ref, get_state, rate_ref, res_ref, skip_ref, out_ref, mult, whole):
     blocks = tok_rows // BLOCK
     zero = jnp.zeros((SUB, LANES), jnp.float32)
     steps = lax.broadcasted_iota(jnp.int32, (SUB, LANES), 0).astype(jnp.float32) + 1.0
@@ -78,7 +89,7 @@
         lanes = pl.ds(pl.multiple_of(g * LANES, LANES), LANES)
         rate = rate_ref[:, lanes]
         coef = res_ref[:, lanes]
-        entering = in_ref[:, lanes]
+        entering = get_state(g, lanes)
         for n in range(blocks):
             state = ends_ref[n * ORDER : (n + 1) * ORDER, lanes] + jnp.exp(-float(BLOCK * n) * rate) * entering
             state = coef * state
@@ -102,6 +113,13 @@
             out_ref[rows, lanes] = gated.astype(jnp.bfloat16)
         return carry
 
+    return group
+
+
+def gate_kernel(tok_rows, width, q_ref, v_ref, conv_ref, ends_ref, in_ref, rate_ref, res_ref, skip_ref, out_ref, mult, whole):
+    group = gate_group(
+        tok_rows, q_ref, v_ref, conv_ref, ends_ref, lambda g, lanes: in_ref[:, lanes], rate_ref, res_ref, skip_ref, out_ref, mult, whole
+    )
     lax.fori_loop(0, width // LANES, group, 0)
 
 
@@ -113,6 +131,238 @@
         return decay * state + in_ref[i]
 
     lax.fori_loop(0, count, hop, jnp.zeros_like(decay))
+
+
+def layer_kernel(
+    tok_rows, width, out_width, count,
+    q_ref, v_ref, rate_ref, res_ref, skip_ref, ow_ref, out_ref,
+    conv, ends, gated, other, last, owned, scanned, back, keeps, takes, total, theirs, far,
+    pad, taps, mult_a, mult_b, whole,
+    w_send, w_recv, a_send, a_recv, b_send, b_recv, p_send, p_recv,
+):
+    zs, ys, xs = GRID
+    half = out_width // 2
+    own = width // count
+    groups = width // LANES
+    me = lax.axis_index("seq")
+    core, x, y, z = me % 2, (me // 2) % xs, (me // (2 * xs)) % ys, me // (2 * xs * ys)
+    place = lambda z, y, x: ((z * ys + y) * xs + x) * 2 + core
+    up, flip_y, flip_x = place((z + 1) % zs, y, x), place(z, 1 - y, x), place(z, y, 1 - x)
+    partner = me + 1 - 2 * core
+    mine_cols = pl.ds(pl.multiple_of(core * half, LANES), half)
+    other_cols = pl.ds(pl.multiple_of((1 - core) * half, LANES), half)
+
+    barrier = pltpu.get_barrier_semaphore()
+
+    def greet(d, carry):
+        pl.semaphore_signal(barrier, inc=1, device_id={"seq": (me + d) % count}, device_id_type=MESH)
+        return carry
+
+    lax.fori_loop(1, count, greet, 0)
+    pl.semaphore_wait(barrier, count - 1)
+
+    slot = lambda at: (at[0] * ys + at[1]) * xs + at[2]
+    copies = {}
+
+    def send(kind, at, to, device):
+        buffer = keeps if kind == "k" else takes
+        source = ow_ref.at[:, mine_cols] if kind == "k" and slot(at) == 0 else buffer.at[slot(at)]
+        number = len(copies)
+        copy = pltpu.make_async_remote_copy(
+            src_ref=source, dst_ref=buffer.at[slot(to)], send_sem=w_send.at[number], recv_sem=w_recv.at[number],
+            device_id={"seq": device}, device_id_type=MESH,
+        )
+        copy.start()
+        copies[kind, to] = copy
+
+    def arrived(kind, at):
+        copies[kind, at].wait_recv()
+
+    def first(kind, dz):
+        if kind == "k":
+            send("k", (dz, 0, 0), (dz, 0, 1), flip_x)
+            send("k", (dz, 0, 0), (dz, 1, 0), flip_y)
+        else:
+            send("t", (dz, 0, 0), (dz, 1, 0), flip_y)
+            send("t", (dz, 0, 0), (dz, 0, 1), flip_x)
+        if dz + 1 < zs:
+            send(kind, (dz, 0, 0), (dz + 1, 0, 0), up)
+
+    def second(dz):
+        arrived("k", (dz, 0, 1))
+        send("k", (dz, 0, 1), (dz, 1, 1), flip_y)
+        arrived("t", (dz, 1, 0))
+        send("t", (dz, 1, 0), (dz, 1, 1), flip_x)
+
+    def round_of(dz):
+        for kind in "kt":
+            arrived(kind, (dz, 0, 0))
+            first(kind, dz)
+        second(dz - 1)
+
+    swap_w = pltpu.make_async_remote_copy(
+        src_ref=ow_ref.at[:, other_cols], dst_ref=takes.at[0], send_sem=p_send.at[0], recv_sem=p_recv.at[0],
+        device_id={"seq": partner}, device_id_type=MESH,
+    )
+    swap_w.start()
+    first("k", 0)
+
+    def put_last(g, lanes, state):
+        last[g] = state
+
+    conv_group = local_group(tok_rows, v_ref, rate_ref, res_ref, conv, ends, put_last, pad, taps, mult_a)
+    lax.fori_loop(0, groups // 8, conv_group, 0)
+    swap_w.wait_recv()
+    first("t", 0)
+    lax.fori_loop(groups // 8, groups, conv_group, 0)
+
+    def exchange(source, target, ssem, rsem):
+        def one(d):
+            return pltpu.make_async_remote_copy(
+                src_ref=source.at[(me + d) % count], dst_ref=target.at[me], send_sem=ssem.at[d], recv_sem=rsem.at[d],
+                device_id={"seq": (me + d) % count}, device_id_type=MESH,
+            )
+
+        def from_there(d):
+            return pltpu.make_async_remote_copy(
+                src_ref=source.at[(me + d) % count], dst_ref=target.at[(me + count - d) % count],
+                send_sem=ssem.at[d], recv_sem=rsem.at[d],
+                device_id={"seq": (me + d) % count}, device_id_type=MESH,
+            )
+
+        def start(d, carry):
+            one(d).start()
+            return carry
+
+        def finish(d, carry):
+            from_there(d).wait_recv()
+            return carry
+
+        def sent(d, carry):
+            one(d).wait_send()
+            return carry
+
+        lax.fori_loop(1, count, start, 0)
+        return lambda: lax.fori_loop(1, count, finish, 0), lambda: lax.fori_loop(1, count, sent, 0)
+
+    ready_a, sent_a = exchange(last, owned, a_send, a_recv)
+    owned[me] = last[me]
+    round_of(1)
+    ready_a()
+    decay = jnp.exp(-float(tok_rows) * rate_ref[:, pl.ds(pl.multiple_of(me * own, LANES), own)])
+
+    def hop(i, state):
+        scanned[i] = state
+        return decay * state + owned[i]
+
+    lax.fori_loop(0, count, hop, jnp.zeros_like(decay))
+    ready_b, sent_b = exchange(scanned, back, b_send, b_recv)
+    back[me] = scanned[me]
+    round_of(2)
+    ready_b()
+    gate = gate_group(
+        tok_rows, q_ref, v_ref, conv, ends, lambda g, lanes: back[g], rate_ref, res_ref, skip_ref, gated, mult_b, whole
+    )
+    lax.fori_loop(0, groups, gate, 0)
+    swap_g = pltpu.make_async_remote_copy(
+        src_ref=gated, dst_ref=other, send_sem=p_send.at[1], recv_sem=p_recv.at[1],
+        device_id={"seq": partner}, device_id_type=MESH,
+    )
+    swap_g.start()
+    round_of(3)
+    second(3)
+    swap_g.wait_recv()
+
+    tile = 256
+
+    def multiply(dz):
+        for dy in range(ys):
+            for dx in range(xs):
+                at = (dz, dy, dx)
+                chip = (((z + zs - dz) % zs) * ys + (y + dy) % ys) * xs + (x + dx) % xs
+                near = pl.ds(pl.multiple_of((2 * chip + core) * own, LANES), own)
+                away = pl.ds(pl.multiple_of((2 * chip + 1 - core) * own, LANES), own)
+                left = jnp.concatenate(
+                    [
+                        jnp.concatenate([gated[:, near], gated[:, away]], axis=1),
+                        jnp.concatenate([other[:, near], other[:, away]], axis=1),
+                    ],
+                    axis=0,
+                )
+
+                def column(n, carry):
+                    cols = pl.ds(pl.multiple_of(n * tile, LANES), tile)
+                    if slot(at) == 0:
+                        kept = ow_ref[:, pl.ds(pl.multiple_of(core * half + n * tile, LANES), tile)]
+                    else:
+                        kept = keeps[slot(at), :, cols]
+                    right = jnp.concatenate([kept, takes[slot(at), :, cols]], axis=0)
+                    term = jnp.dot(left, right, preferred_element_type=jnp.float32)
+                    if slot(at) == 0:
+                        total[:, cols] = term
+                    else:
+                        total[:, cols] += term
+                    return carry
+
+                lax.fori_loop(0, half // tile, column, 0)
+
+    for dz in range(zs):
+        for kind, at in (("k", (dz, 1, 0)), ("t", (dz, 0, 1)), ("k", (dz, 1, 1)), ("t", (dz, 1, 1))):
+            arrived(kind, at)
+        multiply(dz)
+
+    theirs[...] = total[tok_rows:, :].astype(jnp.bfloat16)
+    swap_o = pltpu.make_async_remote_copy(
+        src_ref=theirs, dst_ref=far, send_sem=p_send.at[2], recv_sem=p_recv.at[2],
+        device_id={"seq": partner}, device_id_type=MESH,
+    )
+    swap_o.start()
+    out_ref[:, mine_cols] = total[:tok_rows, :].astype(jnp.bfloat16)
+    swap_w.wait_send()
+    swap_g.wait_send()
+    for copy in copies.values():
+        copy.wait_send()
+    sent_a()
+    sent_b()
+    swap_o.wait()
+    out_ref[:, other_cols] = far[...]
+
+
+def layer(q_gate, values_in, rate, coef, skip, out_weight, count):
+    tok_rows, width = q_gate.shape
+    out_width = out_weight.shape[1]
+    half = out_width // 2
+    blocks = tok_rows // BLOCK
+    chips = math.prod(GRID)
+    states = pltpu.VMEM((count, ORDER, width // count), jnp.float32)
+    weights = pltpu.VMEM((chips, out_weight.shape[0], half), jnp.bfloat16)
+    copies = 2 * (chips - 1)
+    dma = lambda n: pltpu.SemaphoreType.DMA((n,))
+    return pl.pallas_call(
+        functools.partial(layer_kernel, tok_rows, width, out_width, count),
+        in_specs=[pl.BlockSpec(memory_space=pltpu.VMEM)] * 6,
+        out_specs=pl.BlockSpec(memory_space=pltpu.VMEM),
+        out_shape=jax.ShapeDtypeStruct((tok_rows, out_width), jnp.bfloat16),
+        scratch_shapes=[
+            pltpu.VMEM((tok_rows, width), jnp.float32),
+            pltpu.VMEM((blocks * ORDER, width), jnp.float32),
+            pltpu.VMEM((tok_rows, width), jnp.bfloat16),
+            pltpu.VMEM((tok_rows, width), jnp.bfloat16),
+            states, states, states, states,
+            weights, weights,
+            pltpu.VMEM((2 * tok_rows, half), jnp.float32),
+            pltpu.VMEM((tok_rows, half), jnp.bfloat16),
+            pltpu.VMEM((tok_rows, half), jnp.bfloat16),
+            pltpu.VMEM((blocks, SUB + BLOCK, LANES), jnp.float32),
+            pltpu.VMEM((BLOCK, LANES), jnp.float32),
+            pltpu.VMEM((PARTS * ORDER, LANES), jnp.float32),
+            pltpu.VMEM((blocks * PARTS * ORDER, LANES), jnp.float32),
+            pltpu.VMEM((ORDER, SUB, LANES), jnp.float32),
+            dma(copies), dma(copies), dma(count), dma(count), dma(count), dma(count), dma(3), dma(3),
+        ],
+        compiler_params=pltpu.CompilerParams(collective_id=0, has_side_effects=True),
+        name="layer",
+    )(q_gate, values_in, rate, coef, skip, out_weight)
 
 
 def on_device(q_gate, values_in, decay_rate, residue, skip_gain, out_weight):
@@ -124,6 +374,11 @@
     core = me % 2
     swap = [(i, i ^ 1) for i in range(count)]
 
+    rate = decay_rate.T
+    coef = residue.T * jnp.sqrt(-jnp.expm1(-2.0 * rate))
+    if count == 2 * math.prod(GRID) and width == count * LANES:
+        return layer(q_gate, values_in, rate, coef, skip_gain[None], out_weight, count)
+
     keep = lax.dynamic_slice_in_dim(out_weight, core * half, half, 1)
     give = lax.dynamic_slice_in_dim(out_weight, (1 - core) * half, half, 1)
     take = lax.ppermute(give, "seq", swap)
@@ -131,8 +386,6 @@
     sides = [list(range(0, count, 2)), list(range(1, count, 2))]
     weights = lax.all_gather(pair, "seq", axis=0, tiled=True, axis_index_groups=sides)
 
-    rate = decay_rate.T
-    coef = residue.T * jnp.sqrt(-jnp.expm1(-2.0 * rate))
     chunk = 1024
     blocks = tok_rows // BLOCK
     grid = (width // chunk,)

time: 150 us -> 94.5 us (0.63)
  waiting for transfers between devices: 76.3 us -> 0 us
  Pallas kernels: 17 us -> 90.6 us
  blocking collectives: 19.4 us -> 0 us
  between operations: 13.4 us -> 0.01 us
  starting transfers between devices: 8.03 us -> 0 us
  matrix products: 6.04 us -> 0 us
  local copies, waits for them, and re-layouts: 5.53 us -> 1.88 us
  other arithmetic: 3.76 us -> 1.89 us
    pallas_call x3 -> x1, Pallas kernels: 17 us -> 90.6 us  [layer(): pl.pallas_call(functools.partial(layer_kernel, tok_rows, width, out_width...]
    all_gather x1 -> x0, waiting for transfers between devices: 58.4 us -> none  [on_device(): lax.all_gather(pair, 'seq', axis=0, tiled=True, axis_index_groups=sides)]
    all_to_all x1 -> x0, blocking collectives: 19.4 us -> none  [on_device(): back = lax.all_to_all(scanned, 'seq', 0, 0, tiled=True)]
    all_to_all x1 -> x0, waiting for transfers between devices: 12.5 us -> none  [on_device(): owned = lax.all_to_all(spread, 'seq', 0, 0, tiled=True)]
    all_to_all x1 -> x0, starting transfers between devices: 7.2 us -> none  [on_device(): owned = lax.all_to_all(spread, 'seq', 0, 0, tiled=True)]
    dot_general x1 -> x0, matrix products: 6.04 us -> none  [on_device(): jnp.dot(both, weights, preferred_element_type=jnp.float32)]
    ppermute x3 -> x0, waiting for transfers between devices: 5.36 us -> none  [the longest x1 2.67 us: on_device(): other = lax.ppermute(gated, 'seq', swap)]
    dynamic_slice x2 -> x0, local copies, waits for them, and re-layouts: 2.36 us -> none  [the longest x1 1.3 us: on_device(): rate_own = lax.dynamic_slice_in_dim(rate, me * own, own, 1)]
  transfers between devices with their start and end apart: 5 -> 0, of which waited for: 5 -> 0; matrix products, arithmetic and copies ran while one was open for 4% -> 0% of each run, Pallas kernels for 11% -> 0%
where the time goes in v2:
time: 94.5 us; the launch traced here: 94.3 us
  Pallas kernels  90.6 us (96%)
  other arithmetic  1.89 us (2%)
  local copies, waits for them, and re-layouts  1.88 us (2%)
    pallas_call x1, Pallas kernels, layer(): pl.pallas_call(functools.partial(layer_kernel, tok_rows, width, out_width...  90.6 us
    mul x1, other arithmetic, on_device(): coef = residue.T * jnp.sqrt(-jnp.expm1(-2.0 * rate))  1.89 us

profile of v2, /device:TPU:0, one launch (start us, length us, event | category | flops | bytes accessed | tf_op | source)
XLA Modules:
  0.0 94.3 jit_solution(5630453398037640779)
XLA Ops:
  0.0 1.9 %bitcast_multiply_fusion.res_ref = f32[16,4096]{1,0:T(8,128)} fusion(f32[4096,16]{0,1:T(8,128)} %param.9, f32[4096,16]{0,1:T(8,128)} %param.8), kind=kLoop, calls=%fused_computation | loop fusion | flops 196608 | bytes 786432 | tf_op jit(solution)/shard_map/mul | solution.py:378
  1.9 90.6 %layer.1 = bf16[128,2048]{1,0:T(8,128)(2,1)} custom-call(bf16[128,4096]{1,0:T(8,128)(2,1)} %q_ref.1, bf16[128,4096]{1,0:T(8,128)(2,1)} %v_ref.1, f32[16,4096]{1,0:T(8,128)} %bitcast.5, f32[16,4096]{1,0:T(8,128)} %bitcast_multiply_fusion.res_ref, f32[1,4096]{1,0:T(1,128)} %bitcast.6, bf16[128,2048]{1,0:T(8,128)(2,1)} %ow_ref.1), custom_call_target="tpu_custom_call" | custom-call | tf_op jit(solution)/shard_map/layer/pallas_call | solution.py:341
  92.5 1.9 %copy.8 = bf16[128,2048]{1,0:T(8,128)(2,1)} copy(bf16[128,2048]{1,0:T(8,128)(2,1)} %layer.1) | data formatting | bytes 1048576
